TPU v7x, 256 devices: a whole 4x4x8 slice. The times are simulated.
256 devices in a mesh: dp: 32 (over y_lo, z, core), seq: 8 (over y_hi, x).
Axes of the slice: x: 4, y: 4 (y_hi: 2, y_lo: 2; y = y_hi * 2 + y_lo), z: 8, core: 2. Of those that a mesh axis runs over, the one named last changes fastest.
Arguments:
- acts: bfloat16 [32768, 4096], P(('dp', 'seq')), may hold values from -24 to 24
- grad_out: bfloat16 [32768, 4096], P('dp', 'seq'), may hold values from -6 to 6
- proj_weight: bfloat16 [4096, 4096], P('dp', 'seq'), may hold values from -0.09375 to 0.09375
Outputs:
- grad_acts: float32 [32768, 4096], P(('dp', 'seq'))
- grad_weight: float32 [4096, 4096], P('dp', 'seq')
All inputs are finite; a program needn't handle non-finite values.
Results may differ from a plain program's by a relative error of at most 0.014.
Values may be sent and summed in bfloat16 or wider, within the bound.
No kernel may reach another device: no remote copies, remote signals or barrier semaphores. Data moves between devices by JAX's collectives and lax.ppermute only.
A program may use at most 64 MiB of HBM per device.

v0:
```python
import jax
import jax.numpy as jnp
from jax import lax
from jax.sharding import Mesh, PartitionSpec as P

AXES = ("ylo", "z", "core", "yhi", "x")
SIZES = (2, 8, 2, 2, 4)
F32 = jnp.float32
BF16 = jnp.bfloat16


def from_x(value, offset):
    return lax.ppermute(value, "x", [((i + offset) % 4, i) for i in range(4)])


def swap(value, axis):
    return lax.ppermute(value, axis, [(0, 1), (1, 0)])


def rank16(ylo, core, x):
    return (ylo * 2 + core) * 4 + x


TO_BLOCK = [
    (rank16(x % 2, x // 2, (x + 2 * ylo + core) % 4), rank16(ylo, core, x))
    for ylo in range(2)
    for core in range(2)
    for x in range(4)
]
TO_OWNER = [(dst, src) for src, dst in TO_BLOCK]


def dot(a, b, contract):
    return lax.dot_general(
        a, b, ((contract[:1], contract[1:]), ((), ())), preferred_element_type=F32
    )


def per_device(acts, grad_out, weight):
    ylo, core = (lax.axis_index("ylo"), lax.axis_index("core"))
    yhi, x = (lax.axis_index("yhi"), lax.axis_index("x"))
    w = lax.ppermute(weight, ("ylo", "core", "x"), TO_BLOCK)
    w_other = swap(w, "ylo")
    w = jnp.concatenate([jnp.where(ylo == 0, w, w_other), jnp.where(ylo == 0, w_other, w)], axis=1)
    w = lax.all_gather(w, "z", axis=0, tiled=True)
    w_other = swap(w, "core")
    w_even = jnp.where(core == 0, w, w_other)
    w_odd = jnp.where(core == 0, w_other, w)
    blocks = acts.reshape(128, 2, 8, 2, 128).transpose(3, 1, 0, 2, 4).reshape(4, 128, 1024)

    def block_of(stack, k):
        return lax.dynamic_index_in_dim(stack, (x + k) % 4, 0, keepdims=False)

    half = jnp.zeros((4, 128, 1024), BF16)
    for k in range(4):
        piece = block_of(blocks, -k)
        piece = from_x(piece, k) if k else piece
        half = lax.dynamic_update_index_in_dim(half, piece, (x + k) % 4, 0)
    other = swap(half, "yhi")
    tokens = jnp.stack([jnp.where(yhi == 0, half, other), jnp.where(yhi == 0, other, half)])
    tokens = tokens.reshape(1024, 1024)
    g0 = grad_out
    g1 = from_x(g0, 1)
    g3 = from_x(g0, -1)
    g2 = jnp.concatenate([from_x(g1[:512], 1), from_x(g3[512:], -1)], axis=0)
    g = [g0, g1, g2, g3]
    terms = [dot(tokens, g_k, (0, 0)).astype(BF16) for g_k in g]
    keep = [jnp.where(core == 0, terms[0], terms[1]), jnp.where(core == 0, terms[2], terms[3])]
    give = [jnp.where(core == 0, terms[1], terms[0]), jnp.where(core == 0, terms[3], terms[2])]
    s = [(a.astype(F32) + swap(b, "core").astype(F32)).astype(BF16) for a, b in zip(keep, give)]
    keep = jnp.where(ylo == 0, s[0], s[1])
    give = jnp.where(ylo == 0, s[1], s[0])
    s = (keep.astype(F32) + swap(give, "ylo").astype(F32)).astype(BF16)
    s = lax.psum_scatter(s, "z", scatter_dimension=0, tiled=True)
    s = lax.ppermute(s, ("ylo", "core", "x"), TO_OWNER)
    grad_weight = s.astype(F32) / jnp.sqrt(F32(32768))
    part = dot(jnp.concatenate([g0, g2], axis=1), w_even, (1, 1))
    part = part + dot(jnp.concatenate([g1, g3], axis=1), w_odd, (1, 1))
    part = part.reshape(2, 512, 1024)
    give = lax.dynamic_index_in_dim(part, 1 - yhi, 0, keepdims=False).astype(BF16)
    mine = lax.dynamic_index_in_dim(part, yhi, 0, keepdims=False)
    mine = mine + swap(give, "yhi").astype(F32)
    mine = mine.reshape(4, 128, 1024)
    out = jnp.zeros((4, 128, 1024), F32)
    for k in range(4):
        piece = block_of(mine, -k)
        piece = from_x(piece.astype(BF16), k).astype(F32) if k else piece
        out = lax.dynamic_update_index_in_dim(out, piece, (x + k) % 4, 0)
    out = out.reshape(2, 2, 128, 8, 128).transpose(2, 1, 3, 0, 4).reshape(128, 4096)
    return (out, grad_weight)


def solution(mesh):
    fine = Mesh(mesh.devices.reshape(SIZES), AXES)
    rows = P(AXES, None)
    blocks = P(("ylo", "z", "core"), ("yhi", "x"))
    return jax.shard_map(
        per_device,
        mesh=fine,
        in_specs=(rows, blocks, blocks),
        out_specs=(rows, blocks),
        check_vma=False,
    )
```

profile of v0, /device:TPU:1, one launch (start us, length us, event | category | flops | bytes accessed | tf_op | source)
XLA Modules:
  0.0 232.7 jit_solution(10514562266721247765)
XLA Ops:
  10.0 3.3 %collective-permute-start.11 = (bf16[128,1024]{1,0:T(8,128)(2,1)}, bf16[128,1024]{1,0:T(8,128)(2,1)S(1)}, u32[]{:S(2)}, u32[]{:S(2)}) collective-permute-start(bf16[128,1024]{1,0:T(8,128)(2,1)} %bitcast.16), channel_id=1, source_target_pairs={{1,0},{2,1},{3,2},{0,3},{5,4},{6,5},{7,6},{4,7},{9,8},{10,9},{11,1... | collective-permute-start | bytes 786440 | tf_op jit(solution)/shard_map/ppermute | solution.py:13
  19.2 7.3 %collective-permute-start.4 = (bf16[128,512]{1,0:T(8,128)(2,1)}, bf16[128,512]{1,0:T(8,128)(2,1)S(1)}, u32[]{:S(2)}, u32[]{:S(2)}) collective-permute-start(bf16[128,512]{1,0:T(8,128)(2,1)} %param.5), channel_id=1, source_target_pairs={{0,0},{129,1},{10,2},{139,3},{1,8},{130,9},{11,10},{136,11},{2,128... | collective-permute-start | bytes 393224 | tf_op jit(solution)/shard_map/ppermute | solution.py:42
  26.5 16.3 %collective-permute-done.12 = bf16[128,1024]{1,0:T(8,128)(2,1)S(1)} collective-permute-done((bf16[128,1024]{1,0:T(8,128)(2,1)}, bf16[128,1024]{1,0:T(8,128)(2,1)S(1)}, u32[]{:S(2)}, u32[]{:S(2)}) %collective-permute-start.12) | collective-permute-done | bytes 262176 | tf_op jit(solution)/shard_map/ppermute | solution.py:13
  42.8 7.1 %collective-permute-done.13 = bf16[128,1024]{1,0:T(8,128)(2,1)S(1)} collective-permute-done((bf16[128,1024]{1,0:T(8,128)(2,1)}, bf16[128,1024]{1,0:T(8,128)(2,1)S(1)}, u32[]{:S(2)}, u32[]{:S(2)}) %collective-permute-start.13) | collective-permute-done | bytes 262176 | tf_op jit(solution)/shard_map/ppermute | solution.py:13
  49.9 3.0 %collective-permute-start.14 = (bf16[4,128,1024]{2,1,0:T(8,128)(2,1)S(1)}, bf16[4,128,1024]{2,1,0:T(8,128)(2,1)S(1)}, u32[]{:S(2)}, u32[]{:S(2)}) collective-permute-start(bf16[4,128,1024]{2,1,0:T(8,128)(2,1)S(1)} %bitcast_dynamic-update-slice_fusion), channel_id=1, source_target_pairs={{0,4},{4,0},{1,5},{5,1},{2,6},{6,2},{3,7},{7,3},{8,12},{12,8},{9,1... | collective-permute-start | bytes 3145736 | tf_op jit(solution)/shard_map/ppermute | solution.py:17
  55.4 21.8 %collective-permute-done.5 = bf16[128,512]{1,0:T(8,128)(2,1)S(1)} collective-permute-done((bf16[128,512]{1,0:T(8,128)(2,1)S(1)}, bf16[128,512]{1,0:T(8,128)(2,1)S(1)}, u32[]{:S(2)}, u32[]{:S(2)}) %collective-permute-start.5) | collective-permute-done | bytes 131104 | tf_op jit(solution)/shard_map/ppermute | solution.py:17
  83.5 2.6 %broadcast_select_fusion.1 = (bf16[1024,512]{1,0:T(8,128)(2,1)}, bf16[1024,512]{1,0:T(8,128)(2,1)}) fusion(bf16[1024,512]{1,0:T(8,128)(2,1)S(1)} %convolution_convert_fusion.3, pred[]{:T(512)S(6)} %eq.35, bf16[1024,1024]{1,0:T(8,128)(2,1)S(1)} %bitcast.60, bf16[1024,512]{1,0:T(8,128)(2,1)S(1)} %copy-done.6), kind=kOutput, calls=%fused_computation.27 | convolution fusion | flops 1074790400 | bytes 6291457 | tf_op jit(solution)/shard_map/dot_general | solution.py:34
  86.1 3.6 %collective-permute-start.15 = (bf16[1024,512]{1,0:T(8,128)(2,1)}, bf16[1024,512]{1,0:T(8,128)(2,1)S(1)}, u32[]{:S(2)}, u32[]{:S(2)}) collective-permute-start(bf16[1024,512]{1,0:T(8,128)(2,1)} %get-tuple-element.20), channel_id=1, source_target_pairs={{0,8},{8,0},{1,9},{9,1},{2,10},{10,2},{3,11},{11,3},{4,12},{12,4},... | collective-permute-start | bytes 3145736 | tf_op jit(solution)/shard_map/ppermute | solution.py:17
  92.4 4.2 %broadcast_select_fusion = (bf16[1024,512]{1,0:T(8,128)(2,1)}, bf16[1024,512]{1,0:T(8,128)(2,1)}) fusion(bf16[1024,512]{1,0:T(8,128)(2,1)S(1)} %convolution_convert_fusion.1, pred[]{:T(512)S(6)} %eq.35, bf16[1024,1024]{1,0:T(8,128)(2,1)S(1)} %bitcast.62, bf16[1024,512]{1,0:T(8,128)(2,1)} %collective-permute-done.2), kind=kOutput, calls=%fused_computation.26 | convolution fusion | flops 1074790400 | bytes 6291457 | tf_op jit(solution)/shard_map/dot_general | solution.py:34
  96.7 4.0 %collective-permute-start.16 = (bf16[1024,512]{1,0:T(8,128)(2,1)}, bf16[1024,512]{1,0:T(8,128)(2,1)S(1)}, u32[]{:S(2)}, u32[]{:S(2)}) collective-permute-start(bf16[1024,512]{1,0:T(8,128)(2,1)} %get-tuple-element.22), channel_id=1, source_target_pairs={{0,8},{8,0},{1,9},{9,1},{2,10},{10,2},{3,11},{11,3},{4,12},{12,4},... | collective-permute-start | bytes 3145736 | tf_op jit(solution)/shard_map/ppermute | solution.py:17
  100.7 16.6 %all-gather.2.cloned.1.call-done = bf16[1024,1024]{1,0:T(8,128)(2,1)} async-done(((bf16[128,1024]{1,0:T(8,128)(2,1)}), bf16[1024,1024]{1,0:T(8,128)(2,1)}) %all-gather.2.cloned.1.call-update) | async-done | bytes 2097168 | tf_op jit(solution)/shard_map/all_gather | solution.py:45
  117.3 4.6 %collective-permute-start.6 = (bf16[1024,1024]{1,0:T(8,128)(2,1)}, bf16[1024,1024]{1,0:T(8,128)(2,1)}, u32[]{:S(2)}, u32[]{:S(2)}) collective-permute-start(bf16[1024,1024]{1,0:T(8,128)(2,1)} %all-gather.2.cloned.1.call-done), channel_id=1, source_target_pairs={{0,8},{8,0},{1,9},{9,1},{2,10},{10,2},{3,11},{11,3},{4,12},{12,4},... | collective-permute-start | bytes 6291464 | tf_op jit(solution)/shard_map/ppermute | solution.py:17
  123.2 4.1 %broadcast_select_fusion.2 = (bf16[1024,512]{1,0:T(8,128)(2,1)}, bf16[1024,512]{1,0:T(8,128)(2,1)S(1)}, bf16[1024,512]{1,0:T(8,128)(2,1)S(1)}) fusion(pred[]{:T(512)S(6)} %eq.36, bf16[1024,512]{1,0:T(8,128)(2,1)} %copy-done.2, bf16[1024,512]{1,0:T(8,128)(2,1)S(1)} %convolution_convert_fusion.3, bf16[1024,512]{1,0:T(8,128)(2,1)} %get-tuple-element.21, ...), kind=kLoop, calls=%fused_computation.28 | loop fusion | flops 5767168 | bytes 9437186 | tf_op jit(solution)/shard_map/jit(_where)/select_n | solution.py:72
  128.3 24.3 %collective-permute-done.17 = bf16[1024,512]{1,0:T(8,128)(2,1)S(1)} collective-permute-done((bf16[1024,512]{1,0:T(8,128)(2,1)}, bf16[1024,512]{1,0:T(8,128)(2,1)S(1)}, u32[]{:S(2)}, u32[]{:S(2)}) %collective-permute-start.17) | collective-permute-done | bytes 1048608 | tf_op jit(solution)/shard_map/ppermute | solution.py:17
  154.0 4.8 %fusion.4 = f32[1024,1024]{1,0:T(8,128)S(1)} fusion(bf16[1024,512]{1,0:T(8,128)(2,1)} %collective-permute-done.2, bf16[1024,512]{1,0:T(8,128)(2,1)} %copy-done.5, bf16[1024,1024]{1,0:T(8,128)(2,1)} %collective-permute-done.6, bf16[1024,1024]{1,0:T(8,128)(2,1)} %all-gather.2.cloned.1.call-done, pred[]{:T(512)S(6)} %eq.35), kind=kOutput, calls=%fused_computation.4 | convolution fusion | flops 2152726528 | bytes 10485761 | tf_op jit(solution)/shard_map/dot_general | solution.py:34
  158.8 4.0 %fusion.12 = f32[1024,1024]{1,0:T(8,128)S(1)} fusion(f32[1024,1024]{1,0:T(8,128)S(1)} %fusion.4, bf16[1024,1024]{1,0:T(8,128)(2,1)S(1)} %copy-done.9, bf16[1024,1024]{1,0:T(8,128)(2,1)} %collective-permute-done.6, pred[]{:T(512)S(6)} %eq.35, bf16[1024,512]{1,0:T(8,128)(2,1)S(1)} %copy-done.8, bf16[1024,512]{1,0:T(8,128)(2,1)S(1)} %copy-done.11), kind=kOutput, calls=%fused_computation.18 | convolution fusion | flops 2153775104 | bytes 14680065 | tf_op jit(solution)/shard_map/dot_general | solution.py:34
  165.0 2.6 %collective-permute-start.7 = (bf16[512,1024]{1,0:T(8,128)(2,1)S(1)}, bf16[512,1024]{1,0:T(8,128)(2,1)S(1)}, u32[]{:S(2)}, u32[]{:S(2)}) collective-permute-start(bf16[512,1024]{1,0:T(8,128)(2,1)S(1)} %fusion.17), channel_id=1, source_target_pairs={{0,4},{4,0},{1,5},{5,1},{2,6},{6,2},{3,7},{7,3},{8,12},{12,8},{9,1... | collective-permute-start | bytes 3145736 | tf_op jit(solution)/shard_map/ppermute | solution.py:17
  167.5 19.4 %reduce-scatter.2.cloned.1.call-done = bf16[128,512]{1,0:T(8,128)(2,1)} async-done(((bf16[1024,512]{1,0:T(8,128)(2,1)}), bf16[128,512]{1,0:T(8,128)(2,1)}) %reduce-scatter.2.cloned.1.call-update) | async-done | bytes 131088 | tf_op jit(solution)/shard_map/reduce_scatter | solution.py:74
  187.0 7.6 %collective-permute-start.18 = (bf16[128,512]{1,0:T(8,128)(2,1)}, bf16[128,512]{1,0:T(8,128)(2,1)S(1)}, u32[]{:S(2)}, u32[]{:S(2)}) collective-permute-start(bf16[128,512]{1,0:T(8,128)(2,1)} %reduce-scatter.2.cloned.1.call-done), channel_id=1, source_target_pairs={{0,0},{1,129},{2,10},{3,139},{8,1},{9,130},{10,11},{11,136},{128,2... | collective-permute-start | bytes 393224 | tf_op jit(solution)/shard_map/ppermute | solution.py:75
  197.4 2.5 %collective-permute-done.18 = bf16[128,512]{1,0:T(8,128)(2,1)S(1)} collective-permute-done((bf16[128,512]{1,0:T(8,128)(2,1)}, bf16[128,512]{1,0:T(8,128)(2,1)S(1)}, u32[]{:S(2)}, u32[]{:S(2)}) %collective-permute-start.18) | collective-permute-done | bytes 131104 | tf_op jit(solution)/shard_map/ppermute | solution.py:75
  202.5 3.3 %collective-permute-done.8 = bf16[128,1024]{1,0:T(8,128)(2,1)} collective-permute-done((bf16[128,1024]{1,0:T(8,128)(2,1)S(1)}, bf16[128,1024]{1,0:T(8,128)(2,1)}, u32[]{:S(2)}, u32[]{:S(2)}) %collective-permute-start.8) | collective-permute-done | bytes 262176 | tf_op jit(solution)/shard_map/ppermute | solution.py:13
  207.0 3.0 %collective-permute-done.9 = bf16[128,1024]{1,0:T(8,128)(2,1)} collective-permute-done((bf16[128,1024]{1,0:T(8,128)(2,1)}, bf16[128,1024]{1,0:T(8,128)(2,1)}, u32[]{:S(2)}, u32[]{:S(2)}) %collective-permute-start.9) | collective-permute-done | bytes 262176 | tf_op jit(solution)/shard_map/ppermute | solution.py:13
  213.0 3.6 %collective-permute-done.10 = bf16[128,1024]{1,0:T(8,128)(2,1)} collective-permute-done((bf16[128,1024]{1,0:T(8,128)(2,1)S(1)}, bf16[128,1024]{1,0:T(8,128)(2,1)}, u32[]{:S(2)}, u32[]{:S(2)}) %collective-permute-start.10) | collective-permute-done | bytes 262176 | tf_op jit(solution)/shard_map/ppermute | solution.py:13
  223.0 2.9 %copy.25 = f32[128,4096]{1,0:T(8,128)} copy(f32[128,4096]{0,1:T(8,128)} %bitcast.52) | data formatting | bytes 4194304
  (91 shorter events, 41.6 us)
Async XLA Ops:
  7.2 110.1 %all-gather.2.cloned.1.call-start = ((), (), s32[]{:S(2)}) async-start(), calls=%async_computation.1 | async-start | bytes 2359296 | tf_op jit(solution)/shard_map/all_gather | solution.py:45
  10.0 9.2 %collective-permute-start.11 = (bf16[128,1024]{1,0:T(8,128)(2,1)}, bf16[128,1024]{1,0:T(8,128)(2,1)S(1)}, u32[]{:S(2)}, u32[]{:S(2)}) collective-permute-start(bf16[128,1024]{1,0:T(8,128)(2,1)} %bitcast.16), channel_id=1, source_target_pairs={{1,0},{2,1},{3,2},{0,3},{5,4},{6,5},{7,6},{4,7},{9,8},{10,9},{11,1... | collective-permute-start | bytes 786440 | tf_op jit(solution)/shard_map/ppermute | solution.py:13
  13.3 64.7 %collective-permute-start = (bf16[1024,512]{1,0:T(8,128)(2,1)}, bf16[1024,512]{1,0:T(8,128)(2,1)S(1)}, u32[]{:S(2)}, u32[]{:S(2)}) collective-permute-start(bf16[1024,512]{1,0:T(8,128)(2,1)} %param.4), channel_id=1, source_target_pairs={{1,0},{2,1},{3,2},{0,3},{5,4},{6,5},{7,6},{4,7},{9,8},{10,9},{11,1... | collective-permute-start | bytes 3145736 | tf_op jit(solution)/shard_map/ppermute | solution.py:13
  13.8 64.3 %collective-permute-start.2 = (bf16[1024,512]{1,0:T(8,128)(2,1)}, bf16[1024,512]{1,0:T(8,128)(2,1)}, u32[]{:S(2)}, u32[]{:S(2)}) collective-permute-start(bf16[1024,512]{1,0:T(8,128)(2,1)} %param.4), channel_id=1, source_target_pairs={{3,0},{0,1},{1,2},{2,3},{7,4},{4,5},{5,6},{6,7},{11,8},{8,9},{9,10... | collective-permute-start | bytes 3145736 | tf_op jit(solution)/shard_map/ppermute | solution.py:13
  15.6 27.2 %collective-permute-start.12 = (bf16[128,1024]{1,0:T(8,128)(2,1)}, bf16[128,1024]{1,0:T(8,128)(2,1)S(1)}, u32[]{:S(2)}, u32[]{:S(2)}) collective-permute-start(bf16[128,1024]{1,0:T(8,128)(2,1)} %bitcast.18), channel_id=1, source_target_pairs={{2,0},{3,1},{0,2},{1,3},{6,4},{7,5},{4,6},{5,7},{10,8},{11,9},{8,1... | collective-permute-start | bytes 786440 | tf_op jit(solution)/shard_map/ppermute | solution.py:13
  17.0 32.9 %collective-permute-start.13 = (bf16[128,1024]{1,0:T(8,128)(2,1)}, bf16[128,1024]{1,0:T(8,128)(2,1)S(1)}, u32[]{:S(2)}, u32[]{:S(2)}) collective-permute-start(bf16[128,1024]{1,0:T(8,128)(2,1)} %bitcast.20), channel_id=1, source_target_pairs={{3,0},{0,1},{1,2},{2,3},{7,4},{4,5},{5,6},{6,7},{11,8},{8,9},{9,10... | collective-permute-start | bytes 786440 | tf_op jit(solution)/shard_map/ppermute | solution.py:13
  19.2 33.8 %collective-permute-start.4 = (bf16[128,512]{1,0:T(8,128)(2,1)}, bf16[128,512]{1,0:T(8,128)(2,1)S(1)}, u32[]{:S(2)}, u32[]{:S(2)}) collective-permute-start(bf16[128,512]{1,0:T(8,128)(2,1)} %param.5), channel_id=1, source_target_pairs={{0,0},{129,1},{10,2},{139,3},{1,8},{130,9},{11,10},{136,11},{2,128... | collective-permute-start | bytes 393224 | tf_op jit(solution)/shard_map/ppermute | solution.py:42
  49.9 30.8 %collective-permute-start.14 = (bf16[4,128,1024]{2,1,0:T(8,128)(2,1)S(1)}, bf16[4,128,1024]{2,1,0:T(8,128)(2,1)S(1)}, u32[]{:S(2)}, u32[]{:S(2)}) collective-permute-start(bf16[4,128,1024]{2,1,0:T(8,128)(2,1)S(1)} %bitcast_dynamic-update-slice_fusion), channel_id=1, source_target_pairs={{0,4},{4,0},{1,5},{5,1},{2,6},{6,2},{3,7},{7,3},{8,12},{12,8},{9,1... | collective-permute-start | bytes 3145736 | tf_op jit(solution)/shard_map/ppermute | solution.py:17
  52.9 24.2 %collective-permute-start.5 = (bf16[128,512]{1,0:T(8,128)(2,1)S(1)}, bf16[128,512]{1,0:T(8,128)(2,1)S(1)}, u32[]{:S(2)}, u32[]{:S(2)}) collective-permute-start(bf16[128,512]{1,0:T(8,128)(2,1)S(1)} %collective-permute-done.4), channel_id=1, source_target_pairs={{0,128},{128,0},{1,129},{129,1},{2,130},{130,2},{3,131},{131,3},{4... | collective-permute-start | bytes 393224 | tf_op jit(solution)/shard_map/ppermute | solution.py:17
  77.9 109.0 %reduce-scatter.2.cloned.1.call-start = ((), (), s32[]{:S(2)}) async-start(), calls=%async_computation.2 | async-start | bytes 1179648 | tf_op jit(solution)/shard_map/reduce_scatter | solution.py:74
  78.1 11.7 %collective-permute-start.1 = (bf16[512,512]{1,0:T(8,128)(2,1)S(1)}, bf16[512,512]{1,0:T(8,128)(2,1)S(1)}, u32[]{:S(2)}, u32[]{:S(2)}) collective-permute-start(bf16[512,512]{1,0:T(8,128)(2,1)S(1)} %slice.8), channel_id=1, source_target_pairs={{1,0},{2,1},{3,2},{0,3},{5,4},{6,5},{7,6},{4,7},{9,8},{10,9},{11,1... | collective-permute-start | bytes 1572872 | tf_op jit(solution)/shard_map/ppermute | solution.py:13
  79.5 11.6 %collective-permute-start.3 = (bf16[512,512]{1,0:T(8,128)(2,1)S(1)}, bf16[512,512]{1,0:T(8,128)(2,1)S(1)}, u32[]{:S(2)}, u32[]{:S(2)}) collective-permute-start(bf16[512,512]{1,0:T(8,128)(2,1)S(1)} %slice.9), channel_id=1, source_target_pairs={{3,0},{0,1},{1,2},{2,3},{7,4},{4,5},{5,6},{6,7},{11,8},{8,9},{9,10... | collective-permute-start | bytes 1572872 | tf_op jit(solution)/shard_map/ppermute | solution.py:13
  86.1 35.8 %collective-permute-start.15 = (bf16[1024,512]{1,0:T(8,128)(2,1)}, bf16[1024,512]{1,0:T(8,128)(2,1)S(1)}, u32[]{:S(2)}, u32[]{:S(2)}) collective-permute-start(bf16[1024,512]{1,0:T(8,128)(2,1)} %get-tuple-element.20), channel_id=1, source_target_pairs={{0,8},{8,0},{1,9},{9,1},{2,10},{10,2},{3,11},{11,3},{4,12},{12,4},... | collective-permute-start | bytes 3145736 | tf_op jit(solution)/shard_map/ppermute | solution.py:17
  96.7 25.2 %collective-permute-start.16 = (bf16[1024,512]{1,0:T(8,128)(2,1)}, bf16[1024,512]{1,0:T(8,128)(2,1)S(1)}, u32[]{:S(2)}, u32[]{:S(2)}) collective-permute-start(bf16[1024,512]{1,0:T(8,128)(2,1)} %get-tuple-element.22), channel_id=1, source_target_pairs={{0,8},{8,0},{1,9},{9,1},{2,10},{10,2},{3,11},{11,3},{4,12},{12,4},... | collective-permute-start | bytes 3145736 | tf_op jit(solution)/shard_map/ppermute | solution.py:17
  117.3 36.7 %collective-permute-start.6 = (bf16[1024,1024]{1,0:T(8,128)(2,1)}, bf16[1024,1024]{1,0:T(8,128)(2,1)}, u32[]{:S(2)}, u32[]{:S(2)}) collective-permute-start(bf16[1024,1024]{1,0:T(8,128)(2,1)} %all-gather.2.cloned.1.call-done), channel_id=1, source_target_pairs={{0,8},{8,0},{1,9},{9,1},{2,10},{10,2},{3,11},{11,3},{4,12},{12,4},... | collective-permute-start | bytes 6291464 | tf_op jit(solution)/shard_map/ppermute | solution.py:17
  127.3 25.2 %collective-permute-start.17 = (bf16[1024,512]{1,0:T(8,128)(2,1)}, bf16[1024,512]{1,0:T(8,128)(2,1)S(1)}, u32[]{:S(2)}, u32[]{:S(2)}) collective-permute-start(bf16[1024,512]{1,0:T(8,128)(2,1)} %get-tuple-element.6), channel_id=1, source_target_pairs={{0,128},{128,0},{1,129},{129,1},{2,130},{130,2},{3,131},{131,3},{4... | collective-permute-start | bytes 3145736 | tf_op jit(solution)/shard_map/ppermute | solution.py:17
  154.0 4.8 %copy-start.8 = (bf16[1024,512]{1,0:T(8,128)(2,1)S(1)}, bf16[1024,512]{1,0:T(8,128)(2,1)}, u32[]{:S(2)}) copy-start(bf16[1024,512]{1,0:T(8,128)(2,1)} %copy-done.7) | copy-start | bytes 3145732
  154.0 4.8 %copy-start.9 = (bf16[1024,1024]{1,0:T(8,128)(2,1)S(1)}, bf16[1024,1024]{1,0:T(8,128)(2,1)}, u32[]{:S(2)}) copy-start(bf16[1024,1024]{1,0:T(8,128)(2,1)} %all-gather.2.cloned.1.call-done) | copy-start | bytes 6291460
  154.0 4.8 %copy-start.11 = (bf16[1024,512]{1,0:T(8,128)(2,1)S(1)}, bf16[1024,512]{1,0:T(8,128)(2,1)}, u32[]{:S(2)}) copy-start(bf16[1024,512]{1,0:T(8,128)(2,1)} %param.4) | copy-start | bytes 3145732
  165.0 29.7 %collective-permute-start.7 = (bf16[512,1024]{1,0:T(8,128)(2,1)S(1)}, bf16[512,1024]{1,0:T(8,128)(2,1)S(1)}, u32[]{:S(2)}, u32[]{:S(2)}) collective-permute-start(bf16[512,1024]{1,0:T(8,128)(2,1)S(1)} %fusion.17), channel_id=1, source_target_pairs={{0,4},{4,0},{1,5},{5,1},{2,6},{6,2},{3,7},{7,3},{8,12},{12,8},{9,1... | collective-permute-start | bytes 3145736 | tf_op jit(solution)/shard_map/ppermute | solution.py:17
  187.0 12.9 %collective-permute-start.18 = (bf16[128,512]{1,0:T(8,128)(2,1)}, bf16[128,512]{1,0:T(8,128)(2,1)S(1)}, u32[]{:S(2)}, u32[]{:S(2)}) collective-permute-start(bf16[128,512]{1,0:T(8,128)(2,1)} %reduce-scatter.2.cloned.1.call-done), channel_id=1, source_target_pairs={{0,0},{1,129},{2,10},{3,139},{8,1},{9,130},{10,11},{11,136},{128,2... | collective-permute-start | bytes 393224 | tf_op jit(solution)/shard_map/ppermute | solution.py:75
  197.4 8.4 %collective-permute-start.8 = (bf16[128,1024]{1,0:T(8,128)(2,1)S(1)}, bf16[128,1024]{1,0:T(8,128)(2,1)}, u32[]{:S(2)}, u32[]{:S(2)}) collective-permute-start(bf16[128,1024]{1,0:T(8,128)(2,1)S(1)} %get-tuple-element.13), channel_id=1, source_target_pairs={{1,0},{2,1},{3,2},{0,3},{5,4},{6,5},{7,6},{4,7},{9,8},{10,9},{11,1... | collective-permute-start | bytes 786440 | tf_op jit(solution)/shard_map/ppermute | solution.py:13
  200.8 9.1 %collective-permute-start.9 = (bf16[128,1024]{1,0:T(8,128)(2,1)}, bf16[128,1024]{1,0:T(8,128)(2,1)}, u32[]{:S(2)}, u32[]{:S(2)}) collective-permute-start(bf16[128,1024]{1,0:T(8,128)(2,1)} %get-tuple-element.12), channel_id=1, source_target_pairs={{2,0},{3,1},{0,2},{1,3},{6,4},{7,5},{4,6},{5,7},{10,8},{11,9},{8,1... | collective-permute-start | bytes 786440 | tf_op jit(solution)/shard_map/ppermute | solution.py:13
  202.3 14.3 %collective-permute-start.10 = (bf16[128,1024]{1,0:T(8,128)(2,1)S(1)}, bf16[128,1024]{1,0:T(8,128)(2,1)}, u32[]{:S(2)}, u32[]{:S(2)}) collective-permute-start(bf16[128,1024]{1,0:T(8,128)(2,1)S(1)} %get-tuple-element.11), channel_id=1, source_target_pairs={{3,0},{0,1},{1,2},{2,3},{7,4},{4,5},{5,6},{6,7},{11,8},{8,9},{9,10... | collective-permute-start | bytes 786440 | tf_op jit(solution)/shard_map/ppermute | solution.py:13
  (9 other events, 16.3 us)
Sparse Core Ops, SparseCore 0:
  78.1 39.1 all-gather.1
  154.1 32.8 reduce-scatter.1
where the time goes:
time: 233 us
  waiting for transfers between devices  119 us (51%)
  starting transfers between devices  46.2 us (20%)
  local copies, waits for them, and re-layouts  20.7 us (9%)
  matrix products  18.2 us (8%)
  between operations  14.6 us (6%)
  other arithmetic  13.8 us (6%)
    ppermute x7, waiting for transfers between devices, swap(): return lax.ppermute(value, axis, [(0, 1), (1, 0)])  46.1 us
    ppermute x10, waiting for transfers between devices, from_x(): return lax.ppermute(value, 'x', [((i + offset) % 4, i) for i in range(4)])  34.6 us
    ppermute x7, starting transfers between devices, swap(): return lax.ppermute(value, axis, [(0, 1), (1, 0)])  21.3 us
    reduce_scatter x1, waiting for transfers between devices, per_device(): s = lax.psum_scatter(s, 'z', scatter_dimension=0, tiled=True)  19.4 us
    dot_general x6, matrix products, dot(): lax.dot_general(a, b, ((contract[:1], contract[1:]), ((), ())), preferred...  18.2 us
    all_gather x1, waiting for transfers between devices, per_device(): w = lax.all_gather(w, 'z', axis=0, tiled=True)  16.6 us
    ppermute x10, starting transfers between devices, from_x(): return lax.ppermute(value, 'x', [((i + offset) % 4, i) for i in range(4)])  9.94 us
    unnamed x27, local copies, waits for them, and re-layouts  9.8 us
  transfers between devices with their start and end apart: 21, of which 11 were waited for; matrix products, arithmetic and copies ran while one was open for 16% of the time, Pallas kernels for 0%

commit v1 on v0

--- a/solution.py
+++ b/solution.py
@@ -42,7 +42,7 @@
     w = lax.ppermute(weight, ("ylo", "core", "x"), TO_BLOCK)
     w_other = swap(w, "ylo")
     w = jnp.concatenate([jnp.where(ylo == 0, w, w_other), jnp.where(ylo == 0, w_other, w)], axis=1)
-    w = lax.all_gather(w, "z", axis=0, tiled=True)
+    w = jnp.concatenate(lax.all_to_all(jnp.stack([w] * lax.axis_size("z")), "z", 0, 0), axis=0)
     w_other = swap(w, "core")
     w_even = jnp.where(core == 0, w, w_other)
     w_odd = jnp.where(core == 0, w_other, w)

time: 233 us -> 245 us (1.052)
  starting transfers between devices: 46.2 us -> 52.1 us
  waiting for transfers between devices: 119 us -> 124 us
    all_to_all x0 -> x1, waiting for transfers between devices: none -> 26 us  [per_device(): lax.all_to_all(jnp.stack([w] * lax.axis_size('z')), 'z', 0, 0)]
    all_gather x1 -> x0, waiting for transfers between devices: 16.6 us -> none  [per_device(): w = lax.all_gather(w, 'z', axis=0, tiled=True)]
    all_to_all x0 -> x1, starting transfers between devices: none -> 8.19 us  [per_device(): lax.all_to_all(jnp.stack([w] * lax.axis_size('z')), 'z', 0, 0)]
    reduce_scatter x1, waiting for transfers between devices: 19.4 us -> 14.8 us  [per_device(): s = lax.psum_scatter(s, 'z', scatter_dimension=0, tiled=True)]
    unnamed x27 -> x25, local copies, waits for them, and re-layouts: 9.8 us -> 9.83 us
  transfers between devices with their start and end apart: 21 -> 21, of which waited for: 11 -> 12; matrix products, arithmetic and copies ran while one was open for 16% -> 15% of each run, Pallas kernels for 0% -> 0%
where the time goes in v1:
time: 245 us; the launch traced here: 244 us
  waiting for transfers between devices  124 us (51%)
  starting transfers between devices  52.1 us (21%)
  local copies, waits for them, and re-layouts  22.3 us (9%)
  matrix products  18.3 us (7%)
  between operations  14.6 us (6%)
  other arithmetic  13 us (5%)
    ppermute x7, waiting for transfers between devices, swap(): return lax.ppermute(value, axis, [(0, 1), (1, 0)])  48.4 us
    ppermute x10, waiting for transfers between devices, from_x(): return lax.ppermute(value, 'x', [((i + offset) % 4, i) for i in range(4)])  33.8 us
    all_to_all x1, waiting for transfers between devices, per_device(): lax.all_to_all(jnp.stack([w] * lax.axis_size('z')), 'z', 0, 0)  26 us
    ppermute x7, starting transfers between devices, swap(): return lax.ppermute(value, axis, [(0, 1), (1, 0)])  18.9 us
    dot_general x6, matrix products, dot(): lax.dot_general(a, b, ((contract[:1], contract[1:]), ((), ())), preferred...  18.3 us
    reduce_scatter x1, waiting for transfers between devices, per_device(): s = lax.psum_scatter(s, 'z', scatter_dimension=0, tiled=True)  14.8 us
    ppermute x10, starting transfers between devices, from_x(): return lax.ppermute(value, 'x', [((i + offset) % 4, i) for i in range(4)])  9.94 us
    unnamed x25, local copies, waits for them, and re-layouts  9.83 us
  transfers between devices with their start and end apart: 21, of which 12 were waited for; matrix products, arithmetic and copies ran while one was open for 15% of the time, Pallas kernels for 0%

profile of v1, /device:TPU:1, one launch (start us, length us, event | category | flops | bytes accessed | tf_op | source)
XLA Modules:
  0.0 244.5 jit_solution(10187919375621214478)
XLA Ops:
  9.9 3.3 %collective-permute-start.11 = (bf16[128,1024]{1,0:T(8,128)(2,1)}, bf16[128,1024]{1,0:T(8,128)(2,1)S(1)}, u32[]{:S(2)}, u32[]{:S(2)}) collective-permute-start(bf16[128,1024]{1,0:T(8,128)(2,1)} %bitcast.17), channel_id=1, source_target_pairs={{1,0},{2,1},{3,2},{0,3},{5,4},{6,5},{7,6},{4,7},{9,8},{10,9},{11,1... | collective-permute-start | bytes 786440 | tf_op jit(solution)/shard_map/ppermute | solution.py:13
  19.1 7.3 %collective-permute-start.4 = (bf16[128,512]{1,0:T(8,128)(2,1)}, bf16[128,512]{1,0:T(8,128)(2,1)S(1)}, u32[]{:S(2)}, u32[]{:S(2)}) collective-permute-start(bf16[128,512]{1,0:T(8,128)(2,1)} %param.5), channel_id=1, source_target_pairs={{0,0},{129,1},{10,2},{139,3},{1,8},{130,9},{11,10},{136,11},{2,128... | collective-permute-start | bytes 393224 | tf_op jit(solution)/shard_map/ppermute | solution.py:42
  26.4 16.3 %collective-permute-done.12 = bf16[128,1024]{1,0:T(8,128)(2,1)S(1)} collective-permute-done((bf16[128,1024]{1,0:T(8,128)(2,1)}, bf16[128,1024]{1,0:T(8,128)(2,1)S(1)}, u32[]{:S(2)}, u32[]{:S(2)}) %collective-permute-start.12) | collective-permute-done | bytes 262176 | tf_op jit(solution)/shard_map/ppermute | solution.py:13
  42.8 7.1 %collective-permute-done.13 = bf16[128,1024]{1,0:T(8,128)(2,1)S(1)} collective-permute-done((bf16[128,1024]{1,0:T(8,128)(2,1)}, bf16[128,1024]{1,0:T(8,128)(2,1)S(1)}, u32[]{:S(2)}, u32[]{:S(2)}) %collective-permute-start.13) | collective-permute-done | bytes 262176 | tf_op jit(solution)/shard_map/ppermute | solution.py:13
  49.9 3.0 %collective-permute-start.14 = (bf16[4,128,1024]{2,1,0:T(8,128)(2,1)S(1)}, bf16[4,128,1024]{2,1,0:T(8,128)(2,1)S(1)}, u32[]{:S(2)}, u32[]{:S(2)}) collective-permute-start(bf16[4,128,1024]{2,1,0:T(8,128)(2,1)S(1)} %bitcast_dynamic-update-slice_fusion), channel_id=1, source_target_pairs={{0,4},{4,0},{1,5},{5,1},{2,6},{6,2},{3,7},{7,3},{8,12},{12,8},{9,1... | collective-permute-start | bytes 3145736 | tf_op jit(solution)/shard_map/ppermute | solution.py:17
  52.9 2.4 collective-permute-start.5
  55.3 21.8 %collective-permute-done.5 = bf16[128,512]{1,0:T(8,128)(2,1)S(1)} collective-permute-done((bf16[128,512]{1,0:T(8,128)(2,1)S(1)}, bf16[128,512]{1,0:T(8,128)(2,1)S(1)}, u32[]{:S(2)}, u32[]{:S(2)}) %collective-permute-start.5) | collective-permute-done | bytes 131104 | tf_op jit(solution)/shard_map/ppermute | solution.py:17
  78.8 8.2 %all-to-all-start = ((bf16[8,128,1024]{2,1,0:T(8,128)(2,1)}), bf16[8,128,1024]{2,1,0:T(8,128)(2,1)}, u32[]{:S(2)}, u32[]{:S(2)}) async-start(bf16[8,128,1024]{2,1,0:T(8,128)(2,1)} %stack.8), calls=%async_computation | async-start | bytes 4194304 | tf_op jit(solution)/shard_map/all_to_all | solution.py:45
  92.4 2.7 %broadcast_select_fusion.1 = (bf16[1024,512]{1,0:T(8,128)(2,1)}, bf16[1024,512]{1,0:T(8,128)(2,1)}) fusion(bf16[1024,512]{1,0:T(8,128)(2,1)S(1)} %convolution_convert_fusion.3, pred[]{:T(512)S(6)} %eq.35, bf16[1024,1024]{1,0:T(8,128)(2,1)S(1)} %bitcast.61, bf16[1024,512]{1,0:T(8,128)(2,1)S(1)} %copy-done.6), kind=kOutput, calls=%fused_computation.27 | convolution fusion | flops 1074790400 | bytes 6291457 | tf_op jit(solution)/shard_map/dot_general | solution.py:34
  95.1 3.9 %collective-permute-start.15 = (bf16[1024,512]{1,0:T(8,128)(2,1)}, bf16[1024,512]{1,0:T(8,128)(2,1)S(1)}, u32[]{:S(2)}, u32[]{:S(2)}) collective-permute-start(bf16[1024,512]{1,0:T(8,128)(2,1)} %get-tuple-element.20), channel_id=1, source_target_pairs={{0,8},{8,0},{1,9},{9,1},{2,10},{10,2},{3,11},{11,3},{4,12},{12,4},... | collective-permute-start | bytes 3145736 | tf_op jit(solution)/shard_map/ppermute | solution.py:17
  101.3 4.3 %broadcast_select_fusion = (bf16[1024,512]{1,0:T(8,128)(2,1)}, bf16[1024,512]{1,0:T(8,128)(2,1)}) fusion(bf16[1024,512]{1,0:T(8,128)(2,1)S(1)} %convolution_convert_fusion.1, pred[]{:T(512)S(6)} %eq.35, bf16[1024,1024]{1,0:T(8,128)(2,1)S(1)} %bitcast.63, bf16[1024,512]{1,0:T(8,128)(2,1)} %collective-permute-done.2), kind=kOutput, calls=%fused_computation.26 | convolution fusion | flops 1074790400 | bytes 6291457 | tf_op jit(solution)/shard_map/dot_general | solution.py:34
  105.5 4.2 %collective-permute-start.16 = (bf16[1024,512]{1,0:T(8,128)(2,1)}, bf16[1024,512]{1,0:T(8,128)(2,1)S(1)}, u32[]{:S(2)}, u32[]{:S(2)}) collective-permute-start(bf16[1024,512]{1,0:T(8,128)(2,1)} %get-tuple-element.22), channel_id=1, source_target_pairs={{0,8},{8,0},{1,9},{9,1},{2,10},{10,2},{3,11},{11,3},{4,12},{12,4},... | collective-permute-start | bytes 3145736 | tf_op jit(solution)/shard_map/ppermute | solution.py:17
  109.7 26.0 %all-to-all-done = bf16[8,128,1024]{2,1,0:T(8,128)(2,1)} async-done(((bf16[8,128,1024]{2,1,0:T(8,128)(2,1)}), bf16[8,128,1024]{2,1,0:T(8,128)(2,1)}, u32[]{:S(2)}, u32[]{:S(2)}) %all-to-all-start) | async-done | bytes 2097184 | tf_op jit(solution)/shard_map/all_to_all | solution.py:45
  135.7 3.5 %collective-permute-start.6 = (bf16[1024,1024]{1,0:T(8,128)(2,1)}, bf16[1024,1024]{1,0:T(8,128)(2,1)}, u32[]{:S(2)}, u32[]{:S(2)}) collective-permute-start(bf16[1024,1024]{1,0:T(8,128)(2,1)} %bitcast), channel_id=1, source_target_pairs={{0,8},{8,0},{1,9},{9,1},{2,10},{10,2},{3,11},{11,3},{4,12},{12,4},... | collective-permute-start | bytes 6291464 | tf_op jit(solution)/shard_map/ppermute | solution.py:17
  140.6 4.0 %broadcast_select_fusion.2 = (bf16[1024,512]{1,0:T(8,128)(2,1)}, bf16[1024,512]{1,0:T(8,128)(2,1)S(1)}, bf16[1024,512]{1,0:T(8,128)(2,1)S(1)}) fusion(pred[]{:T(512)S(6)} %eq.36, bf16[1024,512]{1,0:T(8,128)(2,1)} %copy-done.2, bf16[1024,512]{1,0:T(8,128)(2,1)S(1)} %convolution_convert_fusion.3, bf16[1024,512]{1,0:T(8,128)(2,1)} %get-tuple-element.21, ...), kind=kLoop, calls=%fused_computation.28 | loop fusion | flops 5767168 | bytes 9437186 | tf_op jit(solution)/shard_map/jit(_where)/select_n | solution.py:72
  144.6 25.2 %collective-permute-done.17 = bf16[1024,512]{1,0:T(8,128)(2,1)S(1)} collective-permute-done((bf16[1024,512]{1,0:T(8,128)(2,1)}, bf16[1024,512]{1,0:T(8,128)(2,1)S(1)}, u32[]{:S(2)}, u32[]{:S(2)}) %collective-permute-start.17) | collective-permute-done | bytes 1048608 | tf_op jit(solution)/shard_map/ppermute | solution.py:17
  171.3 4.7 %fusion.4 = f32[1024,1024]{1,0:T(8,128)S(1)} fusion(bf16[1024,512]{1,0:T(8,128)(2,1)} %collective-permute-done.2, bf16[1024,512]{1,0:T(8,128)(2,1)} %copy-done.5, bf16[1024,1024]{1,0:T(8,128)(2,1)} %collective-permute-done.6, bf16[1024,1024]{1,0:T(8,128)(2,1)} %bitcast, pred[]{:T(512)S(6)} %eq.35), kind=kOutput, calls=%fused_computation.4 | convolution fusion | flops 2152726528 | bytes 10485761 | tf_op jit(solution)/shard_map/dot_general | solution.py:34
  176.0 4.1 %fusion.12 = f32[1024,1024]{1,0:T(8,128)S(1)} fusion(f32[1024,1024]{1,0:T(8,128)S(1)} %fusion.4, bf16[1024,1024]{1,0:T(8,128)(2,1)} %bitcast, bf16[1024,1024]{1,0:T(8,128)(2,1)} %collective-permute-done.6, pred[]{:T(512)S(6)} %eq.35, bf16[1024,512]{1,0:T(8,128)(2,1)S(1)} %copy-done.8, bf16[1024,512]{1,0:T(8,128)(2,1)S(1)} %copy-done.10), kind=kOutput, calls=%fused_computation.18 | convolution fusion | flops 2153775104 | bytes 14680065 | tf_op jit(solution)/shard_map/dot_general | solution.py:34
  184.2 14.8 %reduce-scatter.2.cloned.1.call-done = bf16[128,512]{1,0:T(8,128)(2,1)} async-done(((bf16[1024,512]{1,0:T(8,128)(2,1)}), bf16[128,512]{1,0:T(8,128)(2,1)}) %reduce-scatter.2.cloned.1.call-update) | async-done | bytes 131088 | tf_op jit(solution)/shard_map/reduce_scatter | solution.py:74
  198.9 7.8 %collective-permute-start.18 = (bf16[128,512]{1,0:T(8,128)(2,1)}, bf16[128,512]{1,0:T(8,128)(2,1)S(1)}, u32[]{:S(2)}, u32[]{:S(2)}) collective-permute-start(bf16[128,512]{1,0:T(8,128)(2,1)} %reduce-scatter.2.cloned.1.call-done), channel_id=1, source_target_pairs={{0,0},{1,129},{2,10},{3,139},{8,1},{9,130},{10,11},{11,136},{128,2... | collective-permute-start | bytes 393224 | tf_op jit(solution)/shard_map/ppermute | solution.py:75
  217.3 3.8 %collective-permute-done.9 = bf16[128,1024]{1,0:T(8,128)(2,1)} collective-permute-done((bf16[128,1024]{1,0:T(8,128)(2,1)}, bf16[128,1024]{1,0:T(8,128)(2,1)}, u32[]{:S(2)}, u32[]{:S(2)}) %collective-permute-start.9) | collective-permute-done | bytes 262176 | tf_op jit(solution)/shard_map/ppermute | solution.py:13
  224.1 4.2 %collective-permute-done.10 = bf16[128,1024]{1,0:T(8,128)(2,1)} collective-permute-done((bf16[128,1024]{1,0:T(8,128)(2,1)S(1)}, bf16[128,1024]{1,0:T(8,128)(2,1)}, u32[]{:S(2)}, u32[]{:S(2)}) %collective-permute-start.10) | collective-permute-done | bytes 262176 | tf_op jit(solution)/shard_map/ppermute | solution.py:13
  230.2 2.0 copy.17
  234.8 2.9 %copy.25 = f32[128,4096]{1,0:T(8,128)} copy(f32[128,4096]{0,1:T(8,128)} %bitcast.53) | data formatting | bytes 4194304
  (89 shorter events, 42.4 us)
Async XLA Ops:
  9.9 9.2 %collective-permute-start.11 = (bf16[128,1024]{1,0:T(8,128)(2,1)}, bf16[128,1024]{1,0:T(8,128)(2,1)S(1)}, u32[]{:S(2)}, u32[]{:S(2)}) collective-permute-start(bf16[128,1024]{1,0:T(8,128)(2,1)} %bitcast.17), channel_id=1, source_target_pairs={{1,0},{2,1},{3,2},{0,3},{5,4},{6,5},{7,6},{4,7},{9,8},{10,9},{11,1... | collective-permute-start | bytes 786440 | tf_op jit(solution)/shard_map/ppermute | solution.py:13
  13.2 73.8 %collective-permute-start = (bf16[1024,512]{1,0:T(8,128)(2,1)}, bf16[1024,512]{1,0:T(8,128)(2,1)S(1)}, u32[]{:S(2)}, u32[]{:S(2)}) collective-permute-start(bf16[1024,512]{1,0:T(8,128)(2,1)} %param.4), channel_id=1, source_target_pairs={{1,0},{2,1},{3,2},{0,3},{5,4},{6,5},{7,6},{4,7},{9,8},{10,9},{11,1... | collective-permute-start | bytes 3145736 | tf_op jit(solution)/shard_map/ppermute | solution.py:13
  13.8 73.4 %collective-permute-start.2 = (bf16[1024,512]{1,0:T(8,128)(2,1)}, bf16[1024,512]{1,0:T(8,128)(2,1)}, u32[]{:S(2)}, u32[]{:S(2)}) collective-permute-start(bf16[1024,512]{1,0:T(8,128)(2,1)} %param.4), channel_id=1, source_target_pairs={{3,0},{0,1},{1,2},{2,3},{7,4},{4,5},{5,6},{6,7},{11,8},{8,9},{9,10... | collective-permute-start | bytes 3145736 | tf_op jit(solution)/shard_map/ppermute | solution.py:13
  15.6 27.2 %collective-permute-start.12 = (bf16[128,1024]{1,0:T(8,128)(2,1)}, bf16[128,1024]{1,0:T(8,128)(2,1)S(1)}, u32[]{:S(2)}, u32[]{:S(2)}) collective-permute-start(bf16[128,1024]{1,0:T(8,128)(2,1)} %bitcast.19), channel_id=1, source_target_pairs={{2,0},{3,1},{0,2},{1,3},{6,4},{7,5},{4,6},{5,7},{10,8},{11,9},{8,1... | collective-permute-start | bytes 786440 | tf_op jit(solution)/shard_map/ppermute | solution.py:13
  16.9 32.9 %collective-permute-start.13 = (bf16[128,1024]{1,0:T(8,128)(2,1)}, bf16[128,1024]{1,0:T(8,128)(2,1)S(1)}, u32[]{:S(2)}, u32[]{:S(2)}) collective-permute-start(bf16[128,1024]{1,0:T(8,128)(2,1)} %bitcast.21), channel_id=1, source_target_pairs={{3,0},{0,1},{1,2},{2,3},{7,4},{4,5},{5,6},{6,7},{11,8},{8,9},{9,10... | collective-permute-start | bytes 786440 | tf_op jit(solution)/shard_map/ppermute | solution.py:13
  19.1 33.8 %collective-permute-start.4 = (bf16[128,512]{1,0:T(8,128)(2,1)}, bf16[128,512]{1,0:T(8,128)(2,1)S(1)}, u32[]{:S(2)}, u32[]{:S(2)}) collective-permute-start(bf16[128,512]{1,0:T(8,128)(2,1)} %param.5), channel_id=1, source_target_pairs={{0,0},{129,1},{10,2},{139,3},{1,8},{130,9},{11,10},{136,11},{2,128... | collective-permute-start | bytes 393224 | tf_op jit(solution)/shard_map/ppermute | solution.py:42
  49.9 39.9 %collective-permute-start.14 = (bf16[4,128,1024]{2,1,0:T(8,128)(2,1)S(1)}, bf16[4,128,1024]{2,1,0:T(8,128)(2,1)S(1)}, u32[]{:S(2)}, u32[]{:S(2)}) collective-permute-start(bf16[4,128,1024]{2,1,0:T(8,128)(2,1)S(1)} %bitcast_dynamic-update-slice_fusion), channel_id=1, source_target_pairs={{0,4},{4,0},{1,5},{5,1},{2,6},{6,2},{3,7},{7,3},{8,12},{12,8},{9,1... | collective-permute-start | bytes 3145736 | tf_op jit(solution)/shard_map/ppermute | solution.py:17
  52.9 24.2 %collective-permute-start.5 = (bf16[128,512]{1,0:T(8,128)(2,1)S(1)}, bf16[128,512]{1,0:T(8,128)(2,1)S(1)}, u32[]{:S(2)}, u32[]{:S(2)}) collective-permute-start(bf16[128,512]{1,0:T(8,128)(2,1)S(1)} %collective-permute-done.4), channel_id=1, source_target_pairs={{0,128},{128,0},{1,129},{129,1},{2,130},{130,2},{3,131},{131,3},{4... | collective-permute-start | bytes 393224 | tf_op jit(solution)/shard_map/ppermute | solution.py:17
  78.8 57.0 %all-to-all-start = ((bf16[8,128,1024]{2,1,0:T(8,128)(2,1)}), bf16[8,128,1024]{2,1,0:T(8,128)(2,1)}, u32[]{:S(2)}, u32[]{:S(2)}) async-start(bf16[8,128,1024]{2,1,0:T(8,128)(2,1)} %stack.8), calls=%async_computation | async-start | bytes 4194304 | tf_op jit(solution)/shard_map/all_to_all | solution.py:45
  86.9 112.0 %reduce-scatter.2.cloned.1.call-start = ((), (), s32[]{:S(2)}) async-start(), calls=%async_computation.2 | async-start | bytes 1179648 | tf_op jit(solution)/shard_map/reduce_scatter | solution.py:74
  87.1 12.0 %collective-permute-start.1 = (bf16[512,512]{1,0:T(8,128)(2,1)S(1)}, bf16[512,512]{1,0:T(8,128)(2,1)S(1)}, u32[]{:S(2)}, u32[]{:S(2)}) collective-permute-start(bf16[512,512]{1,0:T(8,128)(2,1)S(1)} %slice.8), channel_id=1, source_target_pairs={{1,0},{2,1},{3,2},{0,3},{5,4},{6,5},{7,6},{4,7},{9,8},{10,9},{11,1... | collective-permute-start | bytes 1572872 | tf_op jit(solution)/shard_map/ppermute | solution.py:13
  88.5 11.4 %collective-permute-start.3 = (bf16[512,512]{1,0:T(8,128)(2,1)S(1)}, bf16[512,512]{1,0:T(8,128)(2,1)S(1)}, u32[]{:S(2)}, u32[]{:S(2)}) collective-permute-start(bf16[512,512]{1,0:T(8,128)(2,1)S(1)} %slice.9), channel_id=1, source_target_pairs={{3,0},{0,1},{1,2},{2,3},{7,4},{4,5},{5,6},{6,7},{11,8},{8,9},{9,10... | collective-permute-start | bytes 1572872 | tf_op jit(solution)/shard_map/ppermute | solution.py:13
  95.1 44.1 %collective-permute-start.15 = (bf16[1024,512]{1,0:T(8,128)(2,1)}, bf16[1024,512]{1,0:T(8,128)(2,1)S(1)}, u32[]{:S(2)}, u32[]{:S(2)}) collective-permute-start(bf16[1024,512]{1,0:T(8,128)(2,1)} %get-tuple-element.20), channel_id=1, source_target_pairs={{0,8},{8,0},{1,9},{9,1},{2,10},{10,2},{3,11},{11,3},{4,12},{12,4},... | collective-permute-start | bytes 3145736 | tf_op jit(solution)/shard_map/ppermute | solution.py:17
  101.3 4.3 %copy-start.3 = (bf16[1024,512]{1,0:T(8,128)(2,1)}, bf16[1024,512]{1,0:T(8,128)(2,1)S(1)}, u32[]{:S(2)}) copy-start(bf16[1024,512]{1,0:T(8,128)(2,1)S(1)} %convolution_convert_fusion.1) | copy-start | bytes 3145732
  105.5 33.7 %collective-permute-start.16 = (bf16[1024,512]{1,0:T(8,128)(2,1)}, bf16[1024,512]{1,0:T(8,128)(2,1)S(1)}, u32[]{:S(2)}, u32[]{:S(2)}) collective-permute-start(bf16[1024,512]{1,0:T(8,128)(2,1)} %get-tuple-element.22), channel_id=1, source_target_pairs={{0,8},{8,0},{1,9},{9,1},{2,10},{10,2},{3,11},{11,3},{4,12},{12,4},... | collective-permute-start | bytes 3145736 | tf_op jit(solution)/shard_map/ppermute | solution.py:17
  135.7 35.5 %collective-permute-start.6 = (bf16[1024,1024]{1,0:T(8,128)(2,1)}, bf16[1024,1024]{1,0:T(8,128)(2,1)}, u32[]{:S(2)}, u32[]{:S(2)}) collective-permute-start(bf16[1024,1024]{1,0:T(8,128)(2,1)} %bitcast), channel_id=1, source_target_pairs={{0,8},{8,0},{1,9},{9,1},{2,10},{10,2},{3,11},{11,3},{4,12},{12,4},... | collective-permute-start | bytes 6291464 | tf_op jit(solution)/shard_map/ppermute | solution.py:17
  144.6 25.2 %collective-permute-start.17 = (bf16[1024,512]{1,0:T(8,128)(2,1)}, bf16[1024,512]{1,0:T(8,128)(2,1)S(1)}, u32[]{:S(2)}, u32[]{:S(2)}) collective-permute-start(bf16[1024,512]{1,0:T(8,128)(2,1)} %get-tuple-element.6), channel_id=1, source_target_pairs={{0,128},{128,0},{1,129},{129,1},{2,130},{130,2},{3,131},{131,3},{4... | collective-permute-start | bytes 3145736 | tf_op jit(solution)/shard_map/ppermute | solution.py:17
  171.2 4.8 %copy-start.8 = (bf16[1024,512]{1,0:T(8,128)(2,1)S(1)}, bf16[1024,512]{1,0:T(8,128)(2,1)}, u32[]{:S(2)}) copy-start(bf16[1024,512]{1,0:T(8,128)(2,1)} %copy-done.7) | copy-start | bytes 3145732
  171.3 4.8 %copy-start.10 = (bf16[1024,512]{1,0:T(8,128)(2,1)S(1)}, bf16[1024,512]{1,0:T(8,128)(2,1)}, u32[]{:S(2)}) copy-start(bf16[1024,512]{1,0:T(8,128)(2,1)} %param.4) | copy-start | bytes 3145732
  182.3 25.8 %collective-permute-start.7 = (bf16[512,1024]{1,0:T(8,128)(2,1)S(1)}, bf16[512,1024]{1,0:T(8,128)(2,1)S(1)}, u32[]{:S(2)}, u32[]{:S(2)}) collective-permute-start(bf16[512,1024]{1,0:T(8,128)(2,1)S(1)} %fusion.17), channel_id=1, source_target_pairs={{0,4},{4,0},{1,5},{5,1},{2,6},{6,2},{3,7},{7,3},{8,12},{12,8},{9,1... | collective-permute-start | bytes 3145736 | tf_op jit(solution)/shard_map/ppermute | solution.py:17
  198.9 13.0 %collective-permute-start.18 = (bf16[128,512]{1,0:T(8,128)(2,1)}, bf16[128,512]{1,0:T(8,128)(2,1)S(1)}, u32[]{:S(2)}, u32[]{:S(2)}) collective-permute-start(bf16[128,512]{1,0:T(8,128)(2,1)} %reduce-scatter.2.cloned.1.call-done), channel_id=1, source_target_pairs={{0,0},{1,129},{2,10},{3,139},{8,1},{9,130},{10,11},{11,136},{128,2... | collective-permute-start | bytes 393224 | tf_op jit(solution)/shard_map/ppermute | solution.py:75
  210.8 5.3 %collective-permute-start.8 = (bf16[128,1024]{1,0:T(8,128)(2,1)S(1)}, bf16[128,1024]{1,0:T(8,128)(2,1)}, u32[]{:S(2)}, u32[]{:S(2)}) collective-permute-start(bf16[128,1024]{1,0:T(8,128)(2,1)S(1)} %get-tuple-element.13), channel_id=1, source_target_pairs={{1,0},{2,1},{3,2},{0,3},{5,4},{6,5},{7,6},{4,7},{9,8},{10,9},{11,1... | collective-permute-start | bytes 786440 | tf_op jit(solution)/shard_map/ppermute | solution.py:13
  212.9 8.2 %collective-permute-start.9 = (bf16[128,1024]{1,0:T(8,128)(2,1)}, bf16[128,1024]{1,0:T(8,128)(2,1)}, u32[]{:S(2)}, u32[]{:S(2)}) collective-permute-start(bf16[128,1024]{1,0:T(8,128)(2,1)} %get-tuple-element.12), channel_id=1, source_target_pairs={{2,0},{3,1},{0,2},{1,3},{6,4},{7,5},{4,6},{5,7},{10,8},{11,9},{8,1... | collective-permute-start | bytes 786440 | tf_op jit(solution)/shard_map/ppermute | solution.py:13
  214.4 14.0 %collective-permute-start.10 = (bf16[128,1024]{1,0:T(8,128)(2,1)S(1)}, bf16[128,1024]{1,0:T(8,128)(2,1)}, u32[]{:S(2)}, u32[]{:S(2)}) collective-permute-start(bf16[128,1024]{1,0:T(8,128)(2,1)S(1)} %get-tuple-element.11), channel_id=1, source_target_pairs={{3,0},{0,1},{1,2},{2,3},{7,4},{4,5},{5,6},{6,7},{11,8},{8,9},{9,10... | collective-permute-start | bytes 786440 | tf_op jit(solution)/shard_map/ppermute | solution.py:13
  (8 other events, 12.1 us)
Sparse Core Ops, SparseCore 0:
  171.4 27.5 reduce-scatter.1
